TPU v7x, 256 devices: a whole 4x4x8 slice. The times are simulated.
256 devices in a mesh: feat: 8 (over z), dom: 32 (over x, y, core).
Axes of the slice: x: 4, y: 4, z: 8, core: 2. Of those that a mesh axis runs over, the one named last changes fastest.
Arguments:
- features: bfloat16 [128, 32768], P('feat', 'dom'), may hold values from -6 to 6
- self_weight: bfloat16 [128, 512], P('feat'), may hold values from -0.5 to 0.5
- neighbor_weight: bfloat16 [128, 512], P('feat'), may hold values from -0.5 to 0.5
- unit_bias: float32 [512], P('feat'), may hold values from -3 to 3
- send_blocks: int32 [32, 32, 4], P('dom'), may hold values from 0 to 7
- send_counts: int32 [32, 32], P('dom'), may hold values from 0 to 4, as said below
- tile_target: int32 [32, 256], P('dom'), may hold values from 0 to 7
- tile_source: int32 [32, 256], P('dom'), may hold values from 0 to 135, as said below
- tile_count: int32 [32], P('dom'), may hold values from 64 to 256, as said below
- tile_weights: bfloat16 [32, 256, 128, 128], P('dom'), may hold values from 0 to 1, as said below
- out_grad: bfloat16 [512, 32768], P('feat', 'dom'), may hold values from -0.119628906 to 0.119628906
Outputs:
- hidden: bfloat16 [512, 32768], P('feat', 'dom')
- self_gradient: float32 [128, 512], P('feat')
- neighbor_gradient: float32 [128, 512], P('feat')
- bias_gradient: float32 [512], P('feat')
Inputs may be any that keep to these rules, and one draw needn't show every extreme that they name: `send_counts`: the diagonal is 0; each partition d fills all 4 slots toward partitions d - 1 and d + 1 (counted round). `tile_count`: at least one partition has all 256 tiles live. `tile_source`: tile 0 of partition d reads slot 8 + ((d + 1) mod 32) * 4, tile 1 reads slot 8 + ((d - 1) mod 32) * 4. `tile_weights`: entries may be 0.
All inputs are finite; a program needn't handle non-finite values.
Results may differ from a plain program's by a relative error of at most 0.005.
Values may be sent and summed in bfloat16 or wider, within the bound.
A program may use at most 64 MiB of HBM per device.

v0:
```python
import jax
import jax.numpy as jnp
from jax import lax
from jax.sharding import PartitionSpec as P

BLK = 128
BMAX = 4


def activate(values):
    return jax.nn.gelu(values, approximate=True)


def body(
    features,
    self_weight,
    neighbor_weight,
    unit_bias,
    send_blocks,
    send_counts,
    tile_target,
    tile_source,
    tile_count,
    tile_weights,
    out_grad,
):
    row_count = features.shape[1]
    unit_width = out_grad.shape[0]
    own_blocks = row_count // BLK
    neighbor_term = jnp.einsum(
        "fh,fr->hr", neighbor_weight, features, preferred_element_type=jnp.float32
    )
    self_term = jnp.einsum("fh,fr->hr", self_weight, features, preferred_element_type=jnp.float32)
    stacked = lax.psum_scatter(
        jnp.concatenate([neighbor_term, self_term], axis=1), "feat", scatter_dimension=0, tiled=True
    )
    projected = stacked[:, :row_count].astype(jnp.bfloat16)
    self_part = stacked[:, row_count:]
    slot_index = jnp.arange(BMAX, dtype=jnp.int32)
    chosen = send_blocks[0].reshape(-1)
    live_slots = (slot_index[None, :] < send_counts[0][:, None]).reshape(-1)
    own_table = projected.reshape(unit_width, own_blocks, BLK)
    outgoing = jnp.take(own_table, chosen, axis=1) * live_slots.astype(jnp.bfloat16)[None, :, None]
    incoming = lax.all_to_all(
        outgoing.reshape(unit_width, -1), "dom", split_axis=1, concat_axis=1, tiled=True
    )
    slot_table = jnp.concatenate([projected, incoming], axis=1).reshape(unit_width, -1, BLK)
    slot_number = slot_table.shape[1]
    weights = tile_weights[0]
    tile_total = weights.shape[0]
    live_tiles = (jnp.arange(tile_total, dtype=jnp.int32) < tile_count[0]).astype(jnp.float32)
    sources = tile_source[0]
    targets = tile_target[0]
    picked = jnp.take(slot_table, sources, axis=1)
    products = (
        jnp.einsum("htc,trc->thr", picked, weights, preferred_element_type=jnp.float32)
        * live_tiles[:, None, None]
    )
    block_sums = jax.ops.segment_sum(products, targets, num_segments=own_blocks)
    aggregate = jnp.transpose(block_sums, (1, 0, 2)).reshape(unit_width, row_count)
    unit_ones = jnp.ones((weights.shape[2],), jnp.bfloat16)
    row_sums = (
        jnp.einsum("trc,c->tr", weights, unit_ones, preferred_element_type=jnp.float32)
        * live_tiles[:, None]
    )
    degree = 1.0 + jax.ops.segment_sum(row_sums, targets, num_segments=own_blocks).reshape(
        row_count
    )
    summed_input = self_part + aggregate / degree[None, :] + unit_bias[:, None]
    hidden, pullback = jax.vjp(activate, summed_input)
    summed_grad = pullback(out_grad.astype(jnp.float32))[0]
    scaled = (summed_grad / degree[None, :]).astype(jnp.bfloat16)
    target_rows = jnp.take(scaled.reshape(unit_width, own_blocks, BLK), targets, axis=1)
    pushed = (
        jnp.einsum("htr,trc->thc", target_rows, weights, preferred_element_type=jnp.float32)
        * live_tiles[:, None, None]
    )
    slot_totals = jax.ops.segment_sum(pushed, sources, num_segments=slot_number)
    returned = lax.all_to_all(
        slot_totals[own_blocks:], "dom", split_axis=0, concat_axis=0, tiled=True
    )
    returned = returned * live_slots.astype(jnp.float32)[:, None, None]
    folded = (
        jax.ops.segment_sum(returned, chosen, num_segments=own_blocks) + slot_totals[:own_blocks]
    )
    neighbor_totals = (
        jnp.transpose(folded, (1, 0, 2)).reshape(unit_width, row_count).astype(jnp.bfloat16)
    )
    narrow_total = summed_grad.astype(jnp.bfloat16)
    bias_part = jnp.sum(summed_grad, axis=1)
    full_narrow, full_neighbor = (
        lax.all_gather(narrow_total, "feat", axis=0, tiled=True),
        lax.all_gather(neighbor_totals, "feat", axis=0, tiled=True),
    )
    self_term = jnp.einsum("fr,hr->fh", features, full_narrow, preferred_element_type=jnp.float32)
    neighbor_term = jnp.einsum(
        "fr,hr->fh", features, full_neighbor, preferred_element_type=jnp.float32
    )
    self_gradient, neighbor_gradient, bias_gradient = lax.psum(
        (self_term, neighbor_term, bias_part), "dom"
    )
    return (hidden.astype(jnp.bfloat16), self_gradient, neighbor_gradient, bias_gradient)


def solution(mesh):
    in_specs = (
        P("feat", "dom"),
        P("feat", None),
        P("feat", None),
        P("feat"),
        P("dom", None, None),
        P("dom", None),
        P("dom", None),
        P("dom", None),
        P("dom"),
        P("dom", None, None, None),
        P("feat", "dom"),
    )
    out_specs = (P("feat", "dom"), P("feat", None), P("feat", None), P("feat"))
    return jax.shard_map(body, mesh=mesh, in_specs=in_specs, out_specs=out_specs, check_vma=False)
```

profile of v0, /device:TPU:1, one launch (start us, length us, event | category | flops | bytes accessed | tf_op | source)
XLA Modules:
  0.0 458.1 jit_solution(16673961788908352427)
XLA Ops:
  7.2 0.7 copy-done
  7.9 1.2 fusion.48
  9.1 1.2 fusion.47
  10.3 2.4 pad_maximum_fusion
  12.7 0.7 copy-done.4
  13.5 0.1 copy.43
  13.6 0.1 broadcast_in_dim.51
  13.7 0.1 reshape_squeeze.6
  13.9 0.1 mul.88
  14.1 58.0 %reduce-scatter.2.cloned.1.call-done = f32[64,2048]{1,0:T(8,128)} async-done(((f32[512,2048]{1,0:T(8,128)}), f32[64,2048]{1,0:T(8,128)}) %reduce-scatter.2.cloned.1.call-update) | async-done | bytes 524304 | tf_op jit(solution)/shard_map/reduce_scatter | solution.py:34
  72.1 1.0 copy_bitcast_fusion.3
  73.0 1.0 gather_fusion
  74.0 2.7 copy.46
  76.7 3.1 gather.15
  79.8 0.2 select_multiply_fusion
  80.0 2.5 copy.47
  82.5 7.5 %all-to-all-start = ((bf16[64,32,512]{2,0,1:T(8,128)(2,1)}), bf16[64,32,512]{2,0,1:T(8,128)(2,1)S(1)}, u32[]{:S(2)}, u32[]{:S(2)}) async-start(bf16[64,32,512]{2,0,1:T(8,128)(2,1)} %copy.47), calls=%async_computation.1 | async-start | bytes 4194304 | tf_op jit(solution)/shard_map/all_to_all | solution.py:44
  90.7 5.7 %fusion.2 = f32[1,256,128]{2,0,1:T(1,128)S(1)} fusion(bf16[1,256,128,128]{3,2,1,0:T(8,128)(2,1)} %param.20), kind=kOutput, calls=%fused_computation.9 | convolution fusion | flops 8388608 | bytes 8519680 | tf_op jit(solution)/shard_map/trc,c->tr/dot_general | solution.py:63
  96.4 2.2 scatter_custom_fusion.1
  98.7 19.6 %all-to-all-done = bf16[64,32,512]{2,0,1:T(8,128)(2,1)S(1)} async-done(((bf16[64,32,512]{2,0,1:T(8,128)(2,1)}), bf16[64,32,512]{2,0,1:T(8,128)(2,1)S(1)}, u32[]{:S(2)}, u32[]{:S(2)}) %all-to-all-start) | async-done | bytes 2097184 | tf_op jit(solution)/shard_map/all_to_all | solution.py:44
  118.3 0.2 copy.58
  118.5 0.6 copy_bitcast_fusion
  119.1 3.1 gather_fusion.1
  122.2 13.6 %broadcast_multiply_fusion.1 = f32[256,64,128]{2,1,0:T(8,128)} fusion(f32[256]{0:T(256)S(1)} %get-tuple-element.14, bf16[1,256,128,128]{3,2,1,0:T(8,128)(2,1)} %param.20, bf16[256,64,128]{2,1,0:T(8,128)(2,1)} %gather_fusion.1, pred[256]{0:T(512)(128)(4,1)S(1)} %get-tuple-element.15), kind=kOutput, calls=%fused_computation.19 | convolution fusion | flops 541065216 | bytes 20972800 | tf_op jit(solution)/shard_map/htc,trc->thr/dot_general | solution.py:56
  135.9 26.2 %scatter_fusion = f32[8,64,128]{2,1,0:T(8,128)S(1)} fusion(f32[8,64,128]{2,1,0:T(8,128)S(1)} %broadcast.124, s32[256]{0:T(256)S(1)} %bitcast.115, f32[256,64,128]{2,1,0:T(8,128)} %broadcast_multiply_fusion.1), kind=kCustom, calls=%fused_computation.3 | custom fusion | flops 2097152 | bytes 25166848 | tf_op jit(solution)/shard_map/scatter-add | solution.py:59
  162.1 1.6 fusion.45
  163.7 0.7 fusion.35
  164.4 3.1 gather_fusion.2
  167.4 10.3 %broadcast_multiply_fusion = f32[256,64,128]{2,1,0:T(8,128)} fusion(f32[256]{0:T(256)S(1)} %get-tuple-element.14, bf16[1,256,128,128]{3,2,1,0:T(8,128)(2,1)} %param.20, bf16[256,64,128]{2,1,0:T(8,128)(2,1)} %gather_fusion.2, pred[256]{0:T(512)(128)(4,1)S(1)} %compare_and_fusion), kind=kOutput, calls=%fused_computation.18 | convolution fusion | flops 541065216 | bytes 20972800 | tf_op jit(solution)/shard_map/htr,trc->thc/dot_general | solution.py:75
  177.8 2.6 broadcast_in_dim.58
  180.4 39.3 %scatter_fusion.1 = f32[136,64,128]{2,1,0:T(8,128)} fusion(f32[136,64,128]{2,1,0:T(8,128)} %broadcast_in_dim.58, s32[256]{0:T(256)S(1)} %bitcast.112, f32[256,64,128]{2,1,0:T(8,128)} %broadcast_multiply_fusion), kind=kCustom, calls=%fused_computation.5 | custom fusion | flops 2097152 | bytes 25166848 | tf_op jit(solution)/shard_map/scatter-add | solution.py:78
  219.8 4.7 %slice.26 = f32[128,64,128]{2,1,0:T(8,128)} slice(f32[136,64,128]{2,1,0:T(8,128)} %scatter_fusion.1), slice={[8:136], [0:64], [0:128]} | slice | bytes 8388608 | tf_op jit(solution)/shard_map/slice | solution.py:80
  224.5 5.3 %all-to-all-start.1 = ((f32[128,64,128]{2,1,0:T(8,128)}), f32[128,64,128]{2,1,0:T(8,128)}, u32[]{:S(2)}, u32[]{:S(2)}) async-start(f32[128,64,128]{2,1,0:T(8,128)} %slice.26), calls=%async_computation.2 | async-start | bytes 8388608 | tf_op jit(solution)/shard_map/all_to_all | solution.py:79
  229.9 0.7 all-gather.3.cloned.1.call-update
  230.6 0.1 reshape.247
  230.7 0.1 reshape.196
  230.8 1.0 slice.25
  231.8 50.3 %all-to-all-done.1 = f32[128,64,128]{2,1,0:T(8,128)} async-done(((f32[128,64,128]{2,1,0:T(8,128)}), f32[128,64,128]{2,1,0:T(8,128)}, u32[]{:S(2)}, u32[]{:S(2)}) %all-to-all-start.1) | async-done | bytes 4194336 | tf_op jit(solution)/shard_map/all_to_all | solution.py:79
  282.1 4.5 broadcast_multiply_fusion.2
  286.6 13.5 %scatter_fusion.2 = f32[8,64,128]{2,1,0:T(8,128)S(1)} fusion(f32[8,64,128]{2,1,0:T(8,128)S(1)} %slice.25, s32[128]{0:T(128)S(1)} %reshape.247, f32[128,64,128]{2,1,0:T(8,128)} %broadcast_multiply_fusion.2), kind=kCustom, calls=%fused_computation.6 | custom fusion | flops 1048576 | bytes 12583424 | tf_op jit(solution)/shard_map/scatter-add | solution.py:84
  300.2 0.7 copy_bitcast_fusion.1
  300.9 2.2 convolution_bitcast_fusion.1
  303.2 29.7 %all-gather.5.cloned.1.call-done = bf16[512,1024]{1,0:T(8,128)(2,1)} async-done(((bf16[64,1024]{1,0:T(8,128)(2,1)}), bf16[512,1024]{1,0:T(8,128)(2,1)}) %all-gather.5.cloned.1.call-update) | async-done | bytes 1048592 | tf_op jit(solution)/shard_map/all_gather | solution.py:93
  332.9 2.2 convolution_bitcast_fusion
  335.1 112.6 %all-reduce.3.cloned.1.call-done = (f32[16,512]{1,0:T(8,128)}, f32[16,512]{1,0:T(8,128)}, f32[64]{0:T(128)}) async-done(((f32[16,512]{1,0:T(8,128)}, f32[16,512]{1,0:T(8,128)}, f32[64]{0:T(128)}), (f32[16,512]{1,0:T(8,128)}, f32[16,512]{1,0:T(8,128)}, f32[64]{0:T(128)})) %all-reduce.3.cloned.1.call-update) | async-done | bytes 65808 | tf_op jit(solution)/shard_map/psum | solution.py:99
  447.7 1.4 copy.85
  449.1 1.4 copy.86
  450.4 1.1 copy.87
  (38 shorter events, 0.6 us)
Async XLA Ops:
  7.2 0.8 copy-start
  7.2 64.9 %reduce-scatter.2.cloned.1.call-start = ((), (), s32[]{:S(2)}) async-start(), calls=%async_computation.3 | async-start | bytes 4718592 | tf_op jit(solution)/shard_map/reduce_scatter | solution.py:34
  12.7 0.7 copy-start.4
  12.7 1.1 copy-start.7
  80.0 10.6 %copy-start.3 = (s32[1,256]{1,0:T(1,128)S(1)}, s32[1,256]{1,0:T(1,128)}, u32[]{:S(2)}) copy-start(s32[1,256]{1,0:T(1,128)} %param.18) | copy-start | bytes 3076
  82.5 35.8 %all-to-all-start = ((bf16[64,32,512]{2,0,1:T(8,128)(2,1)}), bf16[64,32,512]{2,0,1:T(8,128)(2,1)S(1)}, u32[]{:S(2)}, u32[]{:S(2)}) async-start(bf16[64,32,512]{2,0,1:T(8,128)(2,1)} %copy.47), calls=%async_computation.1 | async-start | bytes 4194304 | tf_op jit(solution)/shard_map/all_to_all | solution.py:44
  90.7 5.7 %copy-start.5 = (s32[1,256]{1,0:T(1,128)S(1)}, s32[1,256]{1,0:T(1,128)}, u32[]{:S(2)}) copy-start(s32[1,256]{1,0:T(1,128)} %param.17) | copy-start | bytes 3076
  90.7 8.0 %copy-start.1 = (f32[64,2048]{1,0:T(8,128)S(1)}, f32[64,2048]{1,0:T(8,128)}, u32[]{:S(2)}) copy-start(f32[64,2048]{1,0:T(8,128)} %reduce-scatter.2.cloned.1.call-done) | copy-start | bytes 1572868
  135.8 26.3 %copy-start.2 = (bf16[64,1024]{1,0:T(8,128)(2,1)S(1)}, bf16[64,1024]{1,0:T(8,128)(2,1)}, u32[]{:S(2)}) copy-start(bf16[64,1024]{1,0:T(8,128)(2,1)} %param.21) | copy-start | bytes 393220
  135.8 26.3 %copy-start.6 = (f32[64]{0:T(128)S(1)}, f32[64]{0:T(128)}, u32[]{:S(2)}) copy-start(f32[64]{0:T(128)} %param.14) | copy-start | bytes 772
  224.5 57.6 %all-to-all-start.1 = ((f32[128,64,128]{2,1,0:T(8,128)}), f32[128,64,128]{2,1,0:T(8,128)}, u32[]{:S(2)}, u32[]{:S(2)}) async-start(f32[128,64,128]{2,1,0:T(8,128)} %slice.26), calls=%async_computation.2 | async-start | bytes 8388608 | tf_op jit(solution)/shard_map/all_to_all | solution.py:79
  229.8 71.1 %all-gather.3.cloned.1.call-start = ((), (), s32[]{:S(2)}) async-start(), calls=%async_computation.4 | async-start | bytes 1179648 | tf_op jit(solution)/shard_map/all_gather | solution.py:92
  230.6 102.3 %all-gather.5.cloned.1.call-start = ((), (), s32[]{:S(2)}) async-start(), calls=%async_computation.5 | async-start | bytes 1179648 | tf_op jit(solution)/shard_map/all_gather | solution.py:93
  300.9 146.8 %all-reduce.3.cloned.1.call-start = ((), (), s32[]{:S(2)}) async-start(), calls=%async_computation.6 | async-start | bytes 132096 | tf_op jit(solution)/shard_map/psum | solution.py:99
Sparse Core Ops, SparseCore 0:
  12.9 59.1 reduce-scatter.1
  232.4 33.6 all-gather.2
  301.0 31.8 all-gather.4
  336.9 110.7 all-reduce.2
where the time goes:
time: 460 us; the launch traced here: 458 us
  waiting for transfers between devices  271 us (59%)
  other arithmetic  92.1 us (20%)
  matrix products  36.5 us (8%)
  local copies, waits for them, and re-layouts  30.9 us (7%)
  between operations  14.7 us (3%)
  starting transfers between devices  12.9 us (3%)
    psum x1, waiting for transfers between devices, body(): lax.psum((self_term, neighbor_term, bias_part), 'dom')  113 us
    reduce_scatter x1, waiting for transfers between devices, body(): lax.psum_scatter(jnp.concatenate([neighbor_term, self_term], axis=1), 'fe...  58 us
    all_to_all x1, waiting for transfers between devices, body(): lax.all_to_all(slot_totals[own_blocks:], 'dom', split_axis=0, concat_axis...  50.3 us
    scatter-add x1, other arithmetic, body(): slot_totals = jax.ops.segment_sum(pushed, sources, num_segments=slot_number)  39.3 us
    all_gather x1, waiting for transfers between devices, body(): lax.all_gather(neighbor_totals, 'feat', axis=0, tiled=True)  29.7 us
    scatter-add x1, other arithmetic, body(): block_sums = jax.ops.segment_sum(products, targets, num_segments=own_blocks)  26.2 us
    all_to_all x1, waiting for transfers between devices, body(): lax.all_to_all(outgoing.reshape(unit_width, -1), 'dom', split_axis=1, con...  19.6 us
    dot_general x1, matrix products, body(): jnp.einsum('htc,trc->thr', picked, weights, preferred_element_type=jnp.fl...  13.6 us
  transfers between devices with their start and end apart: 6, of which 5 were waited for; matrix products, arithmetic and copies ran while one was open for 7% of the time, Pallas kernels for 0%

commit v1 on v0

--- a/solution.py
+++ b/solution.py
@@ -90,7 +90,10 @@
     bias_part = jnp.sum(summed_grad, axis=1)
     full_narrow, full_neighbor = (
         lax.all_gather(narrow_total, "feat", axis=0, tiled=True),
-        lax.all_gather(neighbor_totals, "feat", axis=0, tiled=True),
+        jnp.concatenate(
+            lax.all_to_all(jnp.stack([neighbor_totals] * lax.axis_size("feat")), "feat", 0, 0),
+            axis=0,
+        ),
     )
     self_term = jnp.einsum("fr,hr->fh", features, full_narrow, preferred_element_type=jnp.float32)
     neighbor_term = jnp.einsum(

time: 460 us -> 452 us (0.983)
  waiting for transfers between devices: 271 us -> 258 us
    all_gather x1 -> x0, waiting for transfers between devices: 29.7 us -> none  [body(): lax.all_gather(neighbor_totals, 'feat', axis=0, tiled=True)]
    all_to_all x0 -> x1, waiting for transfers between devices: none -> 26.9 us  [body(): lax.all_to_all(jnp.stack([neighbor_totals] * lax.axis_size('feat')), 'fea...]
    psum x1, waiting for transfers between devices: 113 us -> 103 us  [body(): lax.psum((self_term, neighbor_term, bias_part), 'dom')]
where the time goes in v1:
time: 452 us; the launch traced here: 449 us
  waiting for transfers between devices  258 us (57%)
  other arithmetic  91.9 us (20%)
  matrix products  35.2 us (8%)
  local copies, waits for them, and re-layouts  32 us (7%)
  starting transfers between devices  17.1 us (4%)
  between operations  14.7 us (3%)
    psum x1, waiting for transfers between devices, body(): lax.psum((self_term, neighbor_term, bias_part), 'dom')  103 us
    reduce_scatter x1, waiting for transfers between devices, body(): lax.psum_scatter(jnp.concatenate([neighbor_term, self_term], axis=1), 'fe...  58 us
    all_to_all x1, waiting for transfers between devices, body(): lax.all_to_all(slot_totals[own_blocks:], 'dom', split_axis=0, concat_axis...  51 us
    scatter-add x1, other arithmetic, body(): slot_totals = jax.ops.segment_sum(pushed, sources, num_segments=slot_number)  39.7 us
    all_to_all x1, waiting for transfers between devices, body(): lax.all_to_all(jnp.stack([neighbor_totals] * lax.axis_size('feat')), 'fea...  26.9 us
    scatter-add x1, other arithmetic, body(): block_sums = jax.ops.segment_sum(products, targets, num_segments=own_blocks)  26.2 us
    all_to_all x1, waiting for transfers between devices, body(): lax.all_to_all(outgoing.reshape(unit_width, -1), 'dom', split_axis=1, con...  19.6 us
    dot_general x1, matrix products, body(): jnp.einsum('htc,trc->thr', picked, weights, preferred_element_type=jnp.fl...  13.6 us
  transfers between devices with their start and end apart: 6, of which 5 were waited for; matrix products, arithmetic and copies ran while one was open for 7% of the time, Pallas kernels for 0%

profile of v1, /device:TPU:1, one launch (start us, length us, event | category | flops | bytes accessed | tf_op | source)
XLA Modules:
  0.0 449.2 jit_solution(14402341093006155556)
XLA Ops:
  7.2 0.7 copy-done
  7.9 1.2 fusion.48
  9.1 1.2 fusion.47
  10.3 2.4 pad_maximum_fusion
  12.7 0.7 copy-done.4
  13.5 0.1 copy.43
  13.6 0.1 broadcast_in_dim.51
  13.7 0.1 reshape_squeeze.6
  13.9 0.1 mul.88
  14.0 58.0 %reduce-scatter.2.cloned.1.call-done = f32[64,2048]{1,0:T(8,128)} async-done(((f32[512,2048]{1,0:T(8,128)}), f32[64,2048]{1,0:T(8,128)}) %reduce-scatter.2.cloned.1.call-update) | async-done | bytes 524304 | tf_op jit(solution)/shard_map/reduce_scatter | solution.py:34
  72.1 1.0 copy_bitcast_fusion.3
  73.0 1.0 gather_fusion
  74.0 2.7 copy.46
  76.7 3.1 gather.15
  79.8 0.2 select_multiply_fusion
  80.0 2.5 copy.47
  82.5 7.5 %all-to-all-start = ((bf16[64,32,512]{2,0,1:T(8,128)(2,1)}), bf16[64,32,512]{2,0,1:T(8,128)(2,1)S(1)}, u32[]{:S(2)}, u32[]{:S(2)}) async-start(bf16[64,32,512]{2,0,1:T(8,128)(2,1)} %copy.47), calls=%async_computation.1 | async-start | bytes 4194304 | tf_op jit(solution)/shard_map/all_to_all | solution.py:44
  90.7 5.7 %fusion.2 = f32[1,256,128]{2,0,1:T(1,128)S(1)} fusion(bf16[1,256,128,128]{3,2,1,0:T(8,128)(2,1)} %param.20), kind=kOutput, calls=%fused_computation.9 | convolution fusion | flops 8388608 | bytes 8519680 | tf_op jit(solution)/shard_map/trc,c->tr/dot_general | solution.py:63
  96.4 2.2 scatter_custom_fusion.1
  98.7 19.6 %all-to-all-done = bf16[64,32,512]{2,0,1:T(8,128)(2,1)S(1)} async-done(((bf16[64,32,512]{2,0,1:T(8,128)(2,1)}), bf16[64,32,512]{2,0,1:T(8,128)(2,1)S(1)}, u32[]{:S(2)}, u32[]{:S(2)}) %all-to-all-start) | async-done | bytes 2097184 | tf_op jit(solution)/shard_map/all_to_all | solution.py:44
  118.3 0.2 copy.58
  118.5 0.6 copy_bitcast_fusion
  119.1 3.1 gather_fusion.1
  122.2 13.6 %broadcast_multiply_fusion.1 = f32[256,64,128]{2,1,0:T(8,128)} fusion(f32[256]{0:T(256)S(1)} %get-tuple-element.14, bf16[1,256,128,128]{3,2,1,0:T(8,128)(2,1)} %param.20, bf16[256,64,128]{2,1,0:T(8,128)(2,1)} %gather_fusion.1, pred[256]{0:T(512)(128)(4,1)S(1)} %get-tuple-element.15), kind=kOutput, calls=%fused_computation.19 | convolution fusion | flops 541065216 | bytes 20972800 | tf_op jit(solution)/shard_map/htc,trc->thr/dot_general | solution.py:56
  135.8 26.2 %scatter_fusion = f32[8,64,128]{2,1,0:T(8,128)S(1)} fusion(f32[8,64,128]{2,1,0:T(8,128)S(1)} %broadcast.125, s32[256]{0:T(256)S(1)} %bitcast.117, f32[256,64,128]{2,1,0:T(8,128)} %broadcast_multiply_fusion.1), kind=kCustom, calls=%fused_computation.3 | custom fusion | flops 2097152 | bytes 25166848 | tf_op jit(solution)/shard_map/scatter-add | solution.py:59
  162.1 1.6 fusion.45
  163.7 0.7 fusion.35
  164.4 3.1 gather_fusion.2
  167.4 10.4 %broadcast_multiply_fusion = f32[256,64,128]{2,1,0:T(8,128)} fusion(f32[256]{0:T(256)S(1)} %get-tuple-element.14, bf16[1,256,128,128]{3,2,1,0:T(8,128)(2,1)} %param.20, bf16[256,64,128]{2,1,0:T(8,128)(2,1)} %gather_fusion.2, pred[256]{0:T(512)(128)(4,1)S(1)} %compare_and_fusion), kind=kOutput, calls=%fused_computation.18 | convolution fusion | flops 541065216 | bytes 20972800 | tf_op jit(solution)/shard_map/htr,trc->thc/dot_general | solution.py:75
  177.8 2.6 broadcast_in_dim.58
  180.4 39.7 %scatter_fusion.1 = f32[136,64,128]{2,1,0:T(8,128)} fusion(f32[136,64,128]{2,1,0:T(8,128)} %broadcast_in_dim.58, s32[256]{0:T(256)S(1)} %bitcast.114, f32[256,64,128]{2,1,0:T(8,128)} %broadcast_multiply_fusion), kind=kCustom, calls=%fused_computation.5 | custom fusion | flops 2097152 | bytes 25166848 | tf_op jit(solution)/shard_map/scatter-add | solution.py:78
  220.2 4.8 %slice.26 = f32[128,64,128]{2,1,0:T(8,128)} slice(f32[136,64,128]{2,1,0:T(8,128)} %scatter_fusion.1), slice={[8:136], [0:64], [0:128]} | slice | bytes 8388608 | tf_op jit(solution)/shard_map/slice | solution.py:80
  224.9 5.4 %all-to-all-start.1 = ((f32[128,64,128]{2,1,0:T(8,128)}), f32[128,64,128]{2,1,0:T(8,128)}, u32[]{:S(2)}, u32[]{:S(2)}) async-start(f32[128,64,128]{2,1,0:T(8,128)} %slice.26), calls=%async_computation.2 | async-start | bytes 8388608 | tf_op jit(solution)/shard_map/all_to_all | solution.py:79
  230.4 0.1 reshape.254
  230.5 0.1 reshape.203
  230.6 1.0 slice.25
  231.6 51.0 %all-to-all-done.1 = f32[128,64,128]{2,1,0:T(8,128)} async-done(((f32[128,64,128]{2,1,0:T(8,128)}), f32[128,64,128]{2,1,0:T(8,128)}, u32[]{:S(2)}, u32[]{:S(2)}) %all-to-all-start.1) | async-done | bytes 4194336 | tf_op jit(solution)/shard_map/all_to_all | solution.py:79
  282.6 4.5 %broadcast_multiply_fusion.2 = f32[128,64,128]{2,1,0:T(8,128)} fusion(f32[128,64,128]{2,1,0:T(8,128)} %all-to-all-done.1, f32[128]{0:T(128)S(1)} %reshape.203), kind=kLoop, calls=%fused_computation.26 | loop fusion | flops 1048576 | bytes 8389120 | tf_op jit(solution)/shard_map/mul | solution.py:82
  287.1 13.5 %scatter_fusion.2 = f32[8,64,128]{2,1,0:T(8,128)S(1)} fusion(f32[8,64,128]{2,1,0:T(8,128)S(1)} %slice.25, s32[128]{0:T(128)S(1)} %reshape.254, f32[128,64,128]{2,1,0:T(8,128)} %broadcast_multiply_fusion.2), kind=kCustom, calls=%fused_computation.6 | custom fusion | flops 1048576 | bytes 12583424 | tf_op jit(solution)/shard_map/scatter-add | solution.py:84
  300.7 1.1 stack.2
  301.8 4.1 all-to-all-start.2
  305.9 2.2 convolution_bitcast_fusion.1
  308.2 26.9 %all-to-all-done.2 = bf16[8,64,1024]{2,1,0:T(8,128)(2,1)S(1)} async-done(((bf16[8,64,1024]{2,1,0:T(8,128)(2,1)}), bf16[8,64,1024]{2,1,0:T(8,128)(2,1)S(1)}, u32[]{:S(2)}, u32[]{:S(2)}) %all-to-all-start.2) | async-done | bytes 1048608 | tf_op jit(solution)/shard_map/all_to_all | solution.py:94
  335.1 1.0 convolution_bitcast_fusion
  336.1 102.7 %all-reduce.3.cloned.1.call-done = (f32[16,512]{1,0:T(8,128)}, f32[16,512]{1,0:T(8,128)}, f32[64]{0:T(128)}) async-done(((f32[16,512]{1,0:T(8,128)}, f32[16,512]{1,0:T(8,128)}, f32[64]{0:T(128)}), (f32[16,512]{1,0:T(8,128)}, f32[16,512]{1,0:T(8,128)}, f32[64]{0:T(128)})) %all-reduce.3.cloned.1.call-update) | async-done | bytes 65808 | tf_op jit(solution)/shard_map/psum | solution.py:102
  438.8 1.4 copy.85
  440.2 1.4 copy.86
  441.5 1.1 copy.87
  (38 shorter events, 0.5 us)
Async XLA Ops:
  7.2 0.8 copy-start
  7.2 64.9 %reduce-scatter.2.cloned.1.call-start = ((), (), s32[]{:S(2)}) async-start(), calls=%async_computation.4 | async-start | bytes 4718592 | tf_op jit(solution)/shard_map/reduce_scatter | solution.py:34
  12.7 0.7 copy-start.4
  12.7 1.1 copy-start.7
  80.0 10.6 %copy-start.3 = (s32[1,256]{1,0:T(1,128)S(1)}, s32[1,256]{1,0:T(1,128)}, u32[]{:S(2)}) copy-start(s32[1,256]{1,0:T(1,128)} %param.18) | copy-start | bytes 3076
  82.5 35.8 %all-to-all-start = ((bf16[64,32,512]{2,0,1:T(8,128)(2,1)}), bf16[64,32,512]{2,0,1:T(8,128)(2,1)S(1)}, u32[]{:S(2)}, u32[]{:S(2)}) async-start(bf16[64,32,512]{2,0,1:T(8,128)(2,1)} %copy.47), calls=%async_computation.1 | async-start | bytes 4194304 | tf_op jit(solution)/shard_map/all_to_all | solution.py:44
  90.7 5.7 %copy-start.5 = (s32[1,256]{1,0:T(1,128)S(1)}, s32[1,256]{1,0:T(1,128)}, u32[]{:S(2)}) copy-start(s32[1,256]{1,0:T(1,128)} %param.17) | copy-start | bytes 3076
  90.7 8.0 %copy-start.1 = (f32[64,2048]{1,0:T(8,128)S(1)}, f32[64,2048]{1,0:T(8,128)}, u32[]{:S(2)}) copy-start(f32[64,2048]{1,0:T(8,128)} %reduce-scatter.2.cloned.1.call-done) | copy-start | bytes 1572868
  135.8 26.3 %copy-start.2 = (bf16[64,1024]{1,0:T(8,128)(2,1)S(1)}, bf16[64,1024]{1,0:T(8,128)(2,1)}, u32[]{:S(2)}) copy-start(bf16[64,1024]{1,0:T(8,128)(2,1)} %param.21) | copy-start | bytes 393220
  135.8 26.3 %copy-start.6 = (f32[64]{0:T(128)S(1)}, f32[64]{0:T(128)}, u32[]{:S(2)}) copy-start(f32[64]{0:T(128)} %param.14) | copy-start | bytes 772
  224.9 57.7 %all-to-all-start.1 = ((f32[128,64,128]{2,1,0:T(8,128)}), f32[128,64,128]{2,1,0:T(8,128)}, u32[]{:S(2)}, u32[]{:S(2)}) async-start(f32[128,64,128]{2,1,0:T(8,128)} %slice.26), calls=%async_computation.2 | async-start | bytes 8388608 | tf_op jit(solution)/shard_map/all_to_all | solution.py:79
  230.3 75.6 %all-gather.2.cloned.1.call-start = ((), (), s32[]{:S(2)}) async-start(), calls=%async_computation.5 | async-start | bytes 1179648 | tf_op jit(solution)/shard_map/all_gather | solution.py:92
  301.8 33.3 %all-to-all-start.2 = ((bf16[8,64,1024]{2,1,0:T(8,128)(2,1)}), bf16[8,64,1024]{2,1,0:T(8,128)(2,1)S(1)}, u32[]{:S(2)}, u32[]{:S(2)}) async-start(bf16[8,64,1024]{2,1,0:T(8,128)(2,1)} %stack.2), calls=%async_computation.3 | async-start | bytes 2097152 | tf_op jit(solution)/shard_map/all_to_all | solution.py:94
  305.9 132.9 %all-reduce.3.cloned.1.call-start = ((), (), s32[]{:S(2)}) async-start(), calls=%async_computation.6 | async-start | bytes 132096 | tf_op jit(solution)/shard_map/psum | solution.py:102
Sparse Core Ops, SparseCore 0:
  12.9 59.1 reduce-scatter.1
  233.0 33.6 all-gather.1
  336.2 102.5 all-reduce.2
